TPU v7x, 256 devices: a whole 4x4x8 slice. The times are simulated.
256 devices in a mesh: seq: 64 (over z, y_hi, x), head: 4 (over y_lo, core).
Axes of the slice: x: 4, y: 4 (y_hi: 2, y_lo: 2; y = y_hi * 2 + y_lo), z: 8, core: 2. Of those that a mesh axis runs over, the one named last changes fastest.
Arguments:
- queries: bfloat16 [49152, 1536], P('seq', 'head'), may hold values from -24 to 24, as said below
- keys: bfloat16 [49152, 1536], P('seq', 'head'), may hold values from -24 to 24, as said below
- values: bfloat16 [49152, 1536], P('seq', 'head'), may hold values from -24 to 24
- learn_rate: float32 [4, 49152], P('head', 'seq'), may hold values from 0.02 to 0.5
- gate_fast: bfloat16 [4, 384, 384], P('head'), may hold values from -0.3125 to 0.3125
- up_fast: bfloat16 [4, 384, 384], P('head'), may hold values from -0.3125 to 0.3125
- down_fast: bfloat16 [4, 384, 384], P('head'), may hold values from -0.3125 to 0.3125
- ttt_gain: float32 [4, 384], P('head'), may hold values from 0.2 to 0.8
- out_weight: bfloat16 [1536, 1536], P('head'), may hold values from -0.15625 to 0.15625
Outputs:
- mixed: bfloat16 [49152, 1536], P('seq', 'head')
Inputs may be any that keep to these rules, and one draw needn't show every extreme that they name: `queries`: real-valued activations. `keys`: real-valued activations.
All inputs are finite; a program needn't handle non-finite values.
Results may differ from a plain program's by a relative error of at most 0.014.
Values may be sent and summed in bfloat16 or wider, within the bound.
A program may use at most 128 MiB of HBM per device.

v0:
```python
import functools

import jax
import jax.numpy as jnp
from jax import lax
from jax.experimental import pallas as pl
from jax.experimental.pallas import tpu as pltpu
from jax.sharding import Mesh
from jax.sharding import PartitionSpec as P

AXES = ("z", "yh", "x", "yl", "c")
SIZES = (8, 2, 4, 2, 2)
SEQ = ("z", "yh", "x")
HEAD = ("yl", "c")
BLOCKS = 64
PLANE = 16
MESH = pl.DeviceIdType.MESH
BF16 = jnp.bfloat16
F32 = jnp.float32

ns_first = 3.4445
ns_second = -4.775
ns_third = 2.0315
big_negative = -1e30
log2_e = 1.4426950408889634


def dot_nn(left, right):
    return lax.dot_general(left, right, (((1,), (0,)), ((), ())), preferred_element_type=F32)


def dot_nt(left, right):
    return lax.dot_general(left, right, (((1,), (1,)), ((), ())), preferred_element_type=F32)


def dot_tn(left, right):
    return lax.dot_general(left, right, (((0,), (0,)), ((), ())), preferred_element_type=F32)


def halves(wide):
    high = wide.astype(BF16)
    low = (wide - high.astype(F32)).astype(BF16)
    return high, low


def layer(
    q, k, v, lr, weights, gain, out_w,
    out,
    kh, vh, acc, top, total,
    hid, tgt, dgate, dup, part, psend, precv,
    zsend, zrecv, zsum, grad, left, right, stack, new,
    comb, wcol,
    row_s, row_r, d1_s, d1_r, d2_s, d2_r, d3_s, d3_r,
    xs_s, xs_r, zs_s, zs_r, ag_s, ag_r, bc_s, bc_r,
    w_s, w_r, hy_s, hy_r, hc_s, hc_r, hf_s, hf_r,
):
    tok, hd = q.shape
    tile = 256
    tiles = tok // tile
    piece = hd // PLANE

    z = lax.axis_index("z")
    yh = lax.axis_index("yh")
    x = lax.axis_index("x")
    yl = lax.axis_index("yl")
    c = lax.axis_index("c")
    seq = z * 8 + yh * 4 + x
    plane = z * 2 + yh
    head = yl * 2 + c

    def at_seq(by):
        there = lax.rem(seq + by % BLOCKS, BLOCKS)
        return {"z": there // 8, "yh": lax.rem(there, 8) // 4, "x": lax.rem(there, 4)}

    def at_x(by):
        return {"x": lax.rem(x + by % 4, 4)}

    def at_plane(by):
        there = lax.rem(plane + by, PLANE)
        return {"z": there // 2, "yh": lax.rem(there, 2)}

    chip = {"yl": 1 - yl}
    core = {"c": 1 - c}
    across = {"yl": 1 - yl, "c": 1 - c}

    def remote(src, dst, send, recv, where):
        return pltpu.make_async_remote_copy(
            src_ref=src, dst_ref=dst, send_sem=send, recv_sem=recv,
            device_id=where, device_id_type=MESH,
        )

    barrier = pltpu.get_barrier_semaphore()
    greeted = 0
    for where in (
        [at_seq(by) for by in (4, -4, 1, -1)]
        + [at_x(by) for by in (1, 2, 3)]
        + [chip, core, across]
    ):
        pl.semaphore_signal(barrier, inc=1, device_id=where, device_id_type=MESH)
        greeted += 1

    def greet(by, carry):
        pl.semaphore_signal(barrier, inc=1, device_id=at_plane(by), device_id_type=MESH)
        return carry

    lax.fori_loop(1, PLANE, greet, 0)
    pl.semaphore_wait(barrier, greeted + PLANE - 1)

    def rows(i):
        return pl.ds(i * tile, tile)

    own = (k, v)
    held = (kh, vh)

    def row_copy(kind, i):
        n = kind * tiles + i
        return remote(own[kind].at[rows(i)], held[kind].at[3, rows(i)], row_s.at[n], row_r.at[n], at_seq(4))

    def d1_copy(kind, i, first):
        n = kind * tiles + i
        src = own[kind].at[rows(i)] if first else held[kind].at[3, rows(i)]
        return remote(src, held[kind].at[0, rows(i)], d1_s.at[n], d1_r.at[n], at_x(1))

    def d3_copy(kind, i, first):
        n = kind * tiles + i
        src = own[kind].at[rows(i)] if first else held[kind].at[3, rows(i)]
        return remote(src, held[kind].at[2, rows(i)], d3_s.at[n], d3_r.at[n], at_x(-1))

    def d2_copy(kind, i):
        n = kind * tiles + i
        if kind == 0:
            return remote(kh.at[0, rows(i)], kh.at[1, rows(i)], d2_s.at[n], d2_r.at[n], at_seq(1))
        return remote(vh.at[2, rows(i)], vh.at[1, rows(i)], d2_s.at[n], d2_r.at[n], at_seq(-1))

    for kind in (1, 0):
        for i in range(tiles):
            row_copy(kind, i).start()

    @pl.when(x < 3)
    def _():
        for i in range(tiles):
            d1_copy(0, i, True).start()

    @pl.when(x == 0)
    def _():
        for i in range(tiles):
            d3_copy(1, i, True).start()

    def w_copy(n, where, there):
        cols = pl.ds(pl.multiple_of(there * hd, 128), hd)
        return remote(out_w.at[:, cols], wcol.at[head], w_s.at[n], w_r.at[n], where)

    w_copies = (
        w_copy(0, core, yl * 2 + 1 - c),
        w_copy(1, chip, (1 - yl) * 2 + c),
        w_copy(2, across, (1 - yl) * 2 + 1 - c),
    )
    for copy in w_copies:
        copy.start()

    rate = jnp.transpose(jnp.broadcast_to(lr[...], (128, tok)))
    total[...] = rate

    def grad_tile(i, carry):
        at = pl.ds(pl.multiple_of(i * tile, tile), tile)
        k_t = k[at, :]
        gate_k = dot_nn(k_t, weights[0])
        up_k = dot_nn(k_t, weights[1])
        sig = 1.0 / (1.0 + jnp.exp(-gate_k))
        hid[at, :] = (gate_k * sig * up_k).astype(BF16)
        slow = total[at, :]
        slow = jnp.concatenate([slow] * (hd // 128), axis=1)
        target = (-slow * v[at, :].astype(F32)).astype(BF16)
        tgt[at, :] = target
        back = dot_nt(target, weights[2])
        dgate[at, :] = (back * up_k * sig * (1.0 + gate_k * (1.0 - sig))).astype(BF16)
        dup[at, :] = (back * gate_k * sig).astype(BF16)
        return carry

    lax.fori_loop(0, tiles, grad_tile, 0)
    for m, (a, b) in enumerate(((k, dgate), (k, dup), (hid, tgt))):
        mine = dot_tn(a[...], b[...])
        part[m] = mine
        psend[m] = mine.astype(BF16)

    def xs_copy(by):
        m = lax.rem(x + 4 - by, 4)
        to = jnp.minimum(m, 2)
        return m, remote(psend.at[to], precv.at[by - 1], xs_s.at[by - 1], xs_r.at[by - 1], {"x": m})

    for by in (1, 2, 3):
        m, copy = xs_copy(by)

        @pl.when(m < 3)
        def _(copy=copy):
            copy.start()

    @pl.when(x < 3)
    def _():
        for i in range(tiles):
            d1_copy(1, i, True).start()

    @pl.when(x == 0)
    def _():
        for i in range(tiles):
            d3_copy(0, i, True).start()

    scale = log2_e * hd**-0.5

    def attend(keys, values, distance):
        def step(i, carry):
            at = pl.ds(pl.multiple_of(i * tile, tile), tile)
            scores = dot_nt(q[at, :], keys[...]) * scale
            if distance in (0, 4):
                row = lax.broadcasted_iota(jnp.int32, scores.shape, 0) + i * tile
                col = lax.broadcasted_iota(jnp.int32, scores.shape, 1)
                valid = col <= row if distance == 0 else col > row
                scores = jnp.where(valid, scores, big_negative)
            peak = jnp.max(scores, axis=1, keepdims=True)
            if distance == 0:
                expo = jnp.exp2(scores - peak)
                top[at, :] = jnp.broadcast_to(peak, (tile, 128))
                total[at, :] = jnp.broadcast_to(jnp.sum(expo, axis=1, keepdims=True), (tile, 128))
                acc[at, :] = dot_nn(expo.astype(BF16), values[...])
            else:
                old = top[at, :][:, :1]
                peak = jnp.maximum(peak, old)
                shrink = jnp.exp2(old - peak)
                expo = jnp.exp2(scores - peak)
                top[at, :] = jnp.broadcast_to(peak, (tile, 128))
                more = jnp.sum(expo, axis=1, keepdims=True)
                total[at, :] = total[at, :] * shrink + more
                acc[at, :] = acc[at, :] * shrink + dot_nn(expo.astype(BF16), values[...])
            return carry

        lax.fori_loop(0, tiles, step, 0)

    attend(k, v, 0)

    @pl.when(x > 0)
    def _():
        for i in range(tiles):
            d1_copy(0, i, True).wait_recv()
            d2_copy(0, i).start()

    def pass_on(kind):
        for i in range(tiles):
            row_copy(kind, i).wait_recv()

            @pl.when(x == 3)
            def _():
                d1_copy(kind, i, False).start()

            @pl.when(x > 0)
            def _():
                d3_copy(kind, i, False).start()

    pass_on(1)

    owner = x < 3
    which = jnp.minimum(x, 2)

    def zs_copy(by):
        to = lax.rem(plane + by, PLANE)
        return remote(zsend.at[to], zrecv.at[by - 1], zs_s.at[by - 1], zs_r.at[by - 1], at_plane(by))

    def ag_copy(by):
        return remote(zsum, grad.at[plane], ag_s.at[by - 1], ag_r.at[by - 1], at_plane(by))

    def each(fn):
        def go(by, carry):
            fn(by)
            return carry

        lax.fori_loop(1, PLANE, go, 0)

    @pl.when(owner)
    def _():
        for by in (1, 2, 3):
            xs_copy(by)[1].wait_recv()
        whole = part[which] + precv[0].astype(F32) + precv[1].astype(F32) + precv[2].astype(F32)
        zsend[...] = whole.reshape(PLANE, piece, hd)
        each(lambda by: zs_copy(by).start())

    for i in range(tiles):
        d3_copy(1, i, True).wait_recv()
        d2_copy(1, i).start()

    pass_on(0)

    @pl.when(seq >= 4)
    def _():
        attend(kh.at[3], vh.at[3], 4)

    @pl.when(owner)
    def _():
        each(lambda by: zs_copy(by).wait_recv())
        zsum[...] = jnp.sum(zrecv[...], axis=0) + zsend[plane]
        grad[plane] = zsum[...]
        each(lambda by: ag_copy(by).start())

    @pl.when(x == 0)
    def _():
        for i in range(tiles):
            d1_copy(0, i, True).wait_recv()
            d2_copy(0, i).start()

    for i in range(tiles):
        d1_copy(1, i, True).wait_recv()

    @pl.when(seq >= 1)
    def _():
        attend(kh.at[0], vh.at[0], 1)

    for i in range(tiles):
        d3_copy(0, i, True).wait_recv()

    @pl.when(seq >= 3)
    def _():
        attend(kh.at[2], vh.at[2], 3)

    def bc_copy(by):
        return remote(new.at[which], new.at[which], bc_s.at[by - 1], bc_r.at[which], at_x(by))

    @pl.when(owner)
    def _():
        def arrived(by):
            lag = lax.rem(plane + PLANE - by, PLANE)
            remote(zsum, grad.at[lag], ag_s.at[by - 1], ag_r.at[by - 1], at_plane(by)).wait_recv()

        each(arrived)
        whole = grad[...].reshape(hd, hd)
        norm = jnp.sqrt(jnp.sum(whole * whole)) + 1e-07
        part[0] = whole / norm

        def spread(wide):
            high, low = halves(wide)
            left[:, 0:hd] = high
            left[:, hd : 2 * hd] = low
            left[:, 2 * hd : 3 * hd] = high
            return high, low

        def spread_both(wide):
            high, low = spread(wide)
            right[:, 0:hd] = high
            right[:, hd : 2 * hd] = high
            right[:, 2 * hd : 3 * hd] = low
            return high, low

        def sweep(n, carry):
            high, low = spread_both(part[0])
            stack[0:hd] = high
            stack[hd : 2 * hd] = high
            stack[2 * hd : 3 * hd] = low
            square = dot_nt(left[...], right[...])
            part[1] = square
            spread_both(square)
            part[1] = ns_second * part[1] + ns_third * dot_nt(left[...], right[...])
            spread(part[1])
            part[0] = ns_first * part[0] + dot_nn(left[...], stack[...])
            return carry

        lax.fori_loop(0, 5, sweep, 0)
        new[which] = (weights[which].astype(F32) - part[0]).astype(BF16)
        for by in (1, 2, 3):
            bc_copy(by).start()

    for kind in (0, 1):
        for i in range(tiles):
            d2_copy(kind, i).wait_recv()

    @pl.when(seq >= 2)
    def _():
        attend(kh.at[1], vh.at[1], 2)

    for m in range(3):

        @pl.when(x != m)
        def _():
            remote(new.at[m], new.at[m], bc_s.at[0], bc_r.at[m], at_x(1)).wait_recv()

    def hy_copy(i):
        return remote(comb.at[head, rows(i)], comb.at[head, rows(i)], hy_s.at[i], hy_r.at[i], chip)

    def hc_copy(i):
        return remote(comb.at[head, rows(i)], comb.at[head, rows(i)], hc_s.at[i], hc_r.at[i], core)

    far = (1 - yl) * 2 + c

    def hf_copy(i):
        return remote(comb.at[far, rows(i)], comb.at[far, rows(i)], hf_s.at[i], hf_r.at[i], core)

    for i in range(tiles):
        at = rows(i)
        q_t = q[at, :]
        gate_q = dot_nn(q_t, new[0])
        up_q = dot_nn(q_t, new[1])
        q_hidden = (gate_q * (1.0 / (1.0 + jnp.exp(-gate_q))) * up_q).astype(BF16)
        fast = dot_nn(q_hidden, new[2])
        mean = jnp.mean(fast * fast, axis=1, keepdims=True)
        ttt = fast * lax.rsqrt(mean + 1e-06) * gain[...]
        attended = acc[at, :] / total[at, :][:, :1]
        comb[head, at, :] = (attended + ttt).astype(BF16)
        hy_copy(i).start()
        hc_copy(i).start()

    for i in range(tiles):
        hy_copy(i).wait_recv()
        hf_copy(i).start()

    for copy in w_copies:
        copy.wait()
    wcol[head] = out_w[:, pl.ds(pl.multiple_of(head * hd, 128), hd)]

    for i in range(tiles):
        hc_copy(i).wait_recv()
        hf_copy(i).wait_recv()
        at = rows(i)
        mixed = dot_nn(comb[0, at, :], wcol[0])
        for h in range(1, 4):
            mixed += dot_nn(comb[h, at, :], wcol[h])
        out[at, :] = mixed.astype(BF16)

    for kind in (0, 1):
        for i in range(tiles):
            row_copy(kind, i).wait_send()
            d1_copy(kind, i, True).wait_send()
            d2_copy(kind, i).wait_send()
            d3_copy(kind, i, True).wait_send()
    for by in (1, 2, 3):
        m, copy = xs_copy(by)

        @pl.when(m < 3)
        def _(copy=copy):
            copy.wait_send()

    @pl.when(owner)
    def _():
        each(lambda by: zs_copy(by).wait_send())
        each(lambda by: ag_copy(by).wait_send())
        for by in (1, 2, 3):
            bc_copy(by).wait_send()

    for i in range(tiles):
        hy_copy(i).wait_send()
        hc_copy(i).wait_send()
        hf_copy(i).wait_send()


def shards(queries, keys, values, learn_rate, gate_fast, up_fast, down_fast, ttt_gain, out_weight):
    tok, hd = queries.shape
    tiles = tok // 256
    weights = jnp.concatenate([gate_fast, up_fast, down_fast])
    piece = hd // PLANE
    dma = lambda n: pltpu.SemaphoreType.DMA((n,))
    scratch = [
        pltpu.VMEM((4, tok, hd), BF16),
        pltpu.VMEM((4, tok, hd), BF16),
        pltpu.VMEM((tok, hd), F32),
        pltpu.VMEM((tok, 128), F32),
        pltpu.VMEM((tok, 128), F32),
        pltpu.VMEM((tok, hd), BF16),
        pltpu.VMEM((tok, hd), BF16),
        pltpu.VMEM((tok, hd), BF16),
        pltpu.VMEM((tok, hd), BF16),
        pltpu.VMEM((3, hd, hd), F32),
        pltpu.VMEM((3, hd, hd), BF16),
        pltpu.VMEM((3, hd, hd), BF16),
        pltpu.VMEM((PLANE, piece, hd), F32),
        pltpu.VMEM((PLANE - 1, piece, hd), F32),
        pltpu.VMEM((piece, hd), F32),
        pltpu.VMEM((PLANE, piece, hd), F32),
        pltpu.VMEM((hd, 3 * hd), BF16),
        pltpu.VMEM((hd, 3 * hd), BF16),
        pltpu.VMEM((3 * hd, hd), BF16),
        pltpu.VMEM((3, hd, hd), BF16),
        pltpu.VMEM((4, tok, hd), BF16),
        pltpu.VMEM((4, hd, hd), BF16),
    ]
    scratch += [dma(2 * tiles)] * 8
    scratch += [dma(3)] * 2 + [dma(PLANE - 1)] * 4 + [dma(3)] * 2
    scratch += [dma(3)] * 2 + [dma(tiles)] * 6
    vmem = pl.BlockSpec(memory_space=pltpu.VMEM)
    return pl.pallas_call(
        layer,
        out_shape=jax.ShapeDtypeStruct((tok, hd), BF16),
        in_specs=[vmem] * 7,
        out_specs=vmem,
        scratch_shapes=scratch,
        compiler_params=pltpu.CompilerParams(
            collective_id=0, has_side_effects=True, vmem_limit_bytes=56 * 1024 * 1024
        ),
        name="layer",
    )(queries, keys, values, learn_rate, weights, ttt_gain, out_weight)


def solution(mesh):
    torus = Mesh(mesh.devices.reshape(SIZES), AXES)
    in_specs = (
        P(SEQ, HEAD),
        P(SEQ, HEAD),
        P(SEQ, HEAD),
        P(HEAD, SEQ),
        P(HEAD, None, None),
        P(HEAD, None, None),
        P(HEAD, None, None),
        P(HEAD, None),
        P(HEAD, None),
    )
    return jax.shard_map(
        shards, mesh=torus, in_specs=in_specs, out_specs=P(SEQ, HEAD), check_vma=False
    )
```

profile of v0, /device:TPU:53, one launch (start us, length us, event | category | flops | bytes accessed | tf_op | source)
XLA Modules:
  0.0 130.9 jit_solution(8793601296155620582)
XLA Ops:
  0.0 2.2 %pad_maximum_fusion.weights = bf16[3,384,384]{2,1,0:T(8,128)(2,1)} fusion(bf16[1,384,384]{2,1,0:T(8,128)(2,1)} %param.15, bf16[1,384,384]{2,1,0:T(8,128)(2,1)} %param.14, bf16[1,384,384]{2,1,0:T(8,128)(2,1)} %param.13), kind=kLoop, calls=%fused_computation | loop fusion | flops 884736 | bytes 1769472 | tf_op jit(solution)/shard_map/concatenate | solution.py:453
  2.2 126.7 %layer.1 = bf16[768,384]{1,0:T(8,128)(2,1)} custom-call(bf16[768,384]{1,0:T(8,128)(2,1)} %q.1, bf16[768,384]{1,0:T(8,128)(2,1)} %k.1, bf16[768,384]{1,0:T(8,128)(2,1)} %v.1, f32[1,768]{1,0:T(1,128)} %lr.1, bf16[3,384,384]{2,1,0:T(8,128)(2,1)} %pad_maximum_fusion.weights, f32[1,384]{1,0:T(1,128)} %gain.1, bf16[384,1536]{1,0:T(8,128)(2,1)} %out_w.1), custom_call_target="tpu_custom_call" | custom-call | tf_op jit(solution)/shard_map/layer/pallas_call | solution.py:484
  128.9 1.9 %copy.11 = bf16[768,384]{1,0:T(8,128)(2,1)} copy(bf16[768,384]{1,0:T(8,128)(2,1)} %layer.1) | data formatting | bytes 1179648
where the time goes:
time: 132 us; the launch traced here: 131 us
  Pallas kernels  127 us (96%)
  other arithmetic  2.18 us (2%)
  local copies, waits for them, and re-layouts  1.94 us (1%)
    pallas_call x1, Pallas kernels, shards(): pl.pallas_call(layer, out_shape=jax.ShapeDtypeStruct((tok, hd), BF16), in...  127 us

commit v1 on v0

--- a/solution.py
+++ b/solution.py
@@ -14,6 +14,7 @@
 HEAD = ("yl", "c")
 BLOCKS = 64
 PLANE = 16
+PARTS = 6
 MESH = pl.DeviceIdType.MESH
 BF16 = jnp.bfloat16
 F32 = jnp.float32
@@ -44,19 +45,20 @@
 
 
 def layer(
-    q, k, v, lr, weights, gain, out_w,
+    q, k, v, lr, gate_w, up_w, down_w, gain, out_w,
     out,
     kh, vh, acc, top, total,
     hid, tgt, dgate, dup, part, psend, precv,
     zsend, zrecv, zsum, grad, left, right, stack, new,
     comb, wcol,
-    row_s, row_r, d1_s, d1_r, d2_s, d2_r, d3_s, d3_r,
+    row_s, row_r, d1_s, d1_r, d2_s, d2_r, d3_s, d3_r, d4_s,
     xs_s, xs_r, zs_s, zs_r, ag_s, ag_r, bc_s, bc_r,
     w_s, w_r, hy_s, hy_r, hc_s, hc_r, hf_s, hf_r,
 ):
     tok, hd = q.shape
     tile = 256
     tiles = tok // tile
+    chunk = tok // PARTS
     piece = hd // PLANE
 
     z = lax.axis_index("z")
@@ -104,59 +106,35 @@
         return carry
 
     lax.fori_loop(1, PLANE, greet, 0)
-    pl.semaphore_wait(barrier, greeted + PLANE - 1)
 
     def rows(i):
         return pl.ds(i * tile, tile)
 
+    def span(i):
+        return pl.ds(i * chunk, chunk)
+
     own = (k, v)
     held = (kh, vh)
 
     def row_copy(kind, i):
-        n = kind * tiles + i
-        return remote(own[kind].at[rows(i)], held[kind].at[3, rows(i)], row_s.at[n], row_r.at[n], at_seq(4))
+        n = kind * PARTS + i
+        return remote(own[kind].at[span(i)], held[kind].at[3, span(i)], row_s.at[n], row_r.at[n], at_seq(4))
 
     def d1_copy(kind, i, first):
-        n = kind * tiles + i
-        src = own[kind].at[rows(i)] if first else held[kind].at[3, rows(i)]
-        return remote(src, held[kind].at[0, rows(i)], d1_s.at[n], d1_r.at[n], at_x(1))
+        n = kind * PARTS + i
+        src = own[kind].at[span(i)] if first else held[kind].at[3, span(i)]
+        return remote(src, held[kind].at[0, span(i)], d1_s.at[n], d1_r.at[n], at_x(1))
 
     def d3_copy(kind, i, first):
-        n = kind * tiles + i
-        src = own[kind].at[rows(i)] if first else held[kind].at[3, rows(i)]
-        return remote(src, held[kind].at[2, rows(i)], d3_s.at[n], d3_r.at[n], at_x(-1))
+        n = kind * PARTS + i
+        src = own[kind].at[span(i)] if first else held[kind].at[3, span(i)]
+        return remote(src, held[kind].at[2, span(i)], d3_s.at[n], d3_r.at[n], at_x(-1))
 
     def d2_copy(kind, i):
-        n = kind * tiles + i
+        n = kind * PARTS + i
         if kind == 0:
-            return remote(kh.at[0, rows(i)], kh.at[1, rows(i)], d2_s.at[n], d2_r.at[n], at_seq(1))
-        return remote(vh.at[2, rows(i)], vh.at[1, rows(i)], d2_s.at[n], d2_r.at[n], at_seq(-1))
-
-    for kind in (1, 0):
-        for i in range(tiles):
-            row_copy(kind, i).start()
-
-    @pl.when(x < 3)
-    def _():
-        for i in range(tiles):
-            d1_copy(0, i, True).start()
-
-    @pl.when(x == 0)
-    def _():
-        for i in range(tiles):
-            d3_copy(1, i, True).start()
-
-    def w_copy(n, where, there):
-        cols = pl.ds(pl.multiple_of(there * hd, 128), hd)
-        return remote(out_w.at[:, cols], wcol.at[head], w_s.at[n], w_r.at[n], where)
-
-    w_copies = (
-        w_copy(0, core, yl * 2 + 1 - c),
-        w_copy(1, chip, (1 - yl) * 2 + c),
-        w_copy(2, across, (1 - yl) * 2 + 1 - c),
-    )
-    for copy in w_copies:
-        copy.start()
+            return remote(kh.at[0, span(i)], kh.at[1, span(i)], d2_s.at[n], d2_r.at[n], at_seq(1))
+        return remote(vh.at[2, span(i)], vh.at[1, span(i)], d2_s.at[n], d2_r.at[n], at_seq(-1))
 
     rate = jnp.transpose(jnp.broadcast_to(lr[...], (128, tok)))
     total[...] = rate
@@ -164,15 +142,15 @@
     def grad_tile(i, carry):
         at = pl.ds(pl.multiple_of(i * tile, tile), tile)
         k_t = k[at, :]
-        gate_k = dot_nn(k_t, weights[0])
-        up_k = dot_nn(k_t, weights[1])
+        gate_k = dot_nn(k_t, gate_w[0])
+        up_k = dot_nn(k_t, up_w[0])
         sig = 1.0 / (1.0 + jnp.exp(-gate_k))
         hid[at, :] = (gate_k * sig * up_k).astype(BF16)
         slow = total[at, :]
         slow = jnp.concatenate([slow] * (hd // 128), axis=1)
         target = (-slow * v[at, :].astype(F32)).astype(BF16)
         tgt[at, :] = target
-        back = dot_nt(target, weights[2])
+        back = dot_nt(target, down_w[0])
         dgate[at, :] = (back * up_k * sig * (1.0 + gate_k * (1.0 - sig))).astype(BF16)
         dup[at, :] = (back * gate_k * sig).astype(BF16)
         return carry
@@ -182,28 +160,6 @@
         mine = dot_tn(a[...], b[...])
         part[m] = mine
         psend[m] = mine.astype(BF16)
-
-    def xs_copy(by):
-        m = lax.rem(x + 4 - by, 4)
-        to = jnp.minimum(m, 2)
-        return m, remote(psend.at[to], precv.at[by - 1], xs_s.at[by - 1], xs_r.at[by - 1], {"x": m})
-
-    for by in (1, 2, 3):
-        m, copy = xs_copy(by)
-
-        @pl.when(m < 3)
-        def _(copy=copy):
-            copy.start()
-
-    @pl.when(x < 3)
-    def _():
-        for i in range(tiles):
-            d1_copy(1, i, True).start()
-
-    @pl.when(x == 0)
-    def _():
-        for i in range(tiles):
-            d3_copy(0, i, True).start()
 
     scale = log2_e * hd**-0.5
 
@@ -235,30 +191,49 @@
 
         lax.fori_loop(0, tiles, step, 0)
 
+    def w_copy(n, where, there):
+        cols = pl.ds(pl.multiple_of(there * hd, 128), hd)
+        return remote(out_w.at[:, cols], wcol.at[head], w_s.at[n], w_r.at[n], where)
+
+    w_copies = (
+        w_copy(0, core, yl * 2 + 1 - c),
+        w_copy(1, chip, (1 - yl) * 2 + c),
+        w_copy(2, across, (1 - yl) * 2 + 1 - c),
+    )
     attend(k, v, 0)
 
-    @pl.when(x > 0)
-    def _():
-        for i in range(tiles):
-            d1_copy(0, i, True).wait_recv()
-            d2_copy(0, i).start()
-
-    def pass_on(kind):
-        for i in range(tiles):
-            row_copy(kind, i).wait_recv()
-
-            @pl.when(x == 3)
-            def _():
-                d1_copy(kind, i, False).start()
-
-            @pl.when(x > 0)
-            def _():
-                d3_copy(kind, i, False).start()
-
-    pass_on(1)
+    def pass_on(kind, i):
+        row_copy(kind, i).wait_recv()
+
+        @pl.when(x == 3)
+        def _():
+            d1_copy(kind, i, False).start()
+
+        @pl.when(x > 0)
+        def _():
+            d3_copy(kind, i, False).start()
+
+    def send_keys(i):
+        d1_copy(0, i, True).wait_recv()
+        d2_copy(0, i).start()
+
+    def send_values(i):
+        d3_copy(1, i, True).wait_recv()
+
+        @pl.when(x > 0)
+        def _():
+            d2_copy(1, i).start()
+
+    def right_copy(i):
+        return remote(vh.at[0, span(i)], vh.at[1, span(i)], d4_s.at[i], d2_r.at[PARTS + i], at_x(1))
 
     owner = x < 3
     which = jnp.minimum(x, 2)
+
+    def xs_copy(by):
+        m = lax.rem(x + 4 - by, 4)
+        to = jnp.minimum(m, 2)
+        return m, remote(psend.at[to], precv.at[by - 1], xs_s.at[by - 1], xs_r.at[by - 1], {"x": m})
 
     def zs_copy(by):
         to = lax.rem(plane + by, PLANE)
@@ -274,50 +249,88 @@
 
         lax.fori_loop(1, PLANE, go, 0)
 
+    pl.semaphore_wait(barrier, greeted + PLANE - 1)
+
+    for by in (1, 2, 3):
+        m, copy = xs_copy(by)
+
+        @pl.when(m < 3)
+        def _(copy=copy):
+            copy.start()
+
+    for kind in (1, 0):
+        for i in range(PARTS):
+            row_copy(kind, i).start()
+
     @pl.when(owner)
     def _():
         for by in (1, 2, 3):
             xs_copy(by)[1].wait_recv()
         whole = part[which] + precv[0].astype(F32) + precv[1].astype(F32) + precv[2].astype(F32)
-        zsend[...] = whole.reshape(PLANE, piece, hd)
+        part[which] = whole
+        zsend[...] = whole.reshape(PLANE, piece, hd).astype(BF16)
         each(lambda by: zs_copy(by).start())
 
-    for i in range(tiles):
-        d3_copy(1, i, True).wait_recv()
-        d2_copy(1, i).start()
-
-    pass_on(0)
-
-    @pl.when(seq >= 4)
-    def _():
-        attend(kh.at[3], vh.at[3], 4)
+    @pl.when(x < 3)
+    def _():
+        for kind in (0, 1):
+            for i in range(PARTS):
+                d1_copy(kind, i, True).start()
+
+    @pl.when(x == 0)
+    def _():
+        for kind in (1, 0):
+            for i in range(PARTS):
+                d3_copy(kind, i, True).start()
+
+    for i in range(PARTS):
+        pass_on(1, i)
+        if i >= 1:
+            send_values(i - 1)
+
+    send_values(PARTS - 1)
+
+    @pl.when(x > 0)
+    def _():
+        for i in range(PARTS // 2):
+            send_keys(i)
+
+    for i in range(PARTS // 2):
+        pass_on(0, i)
+
+    @pl.when(x > 0)
+    def _():
+        for i in range(PARTS // 2, PARTS):
+            send_keys(i)
 
     @pl.when(owner)
     def _():
         each(lambda by: zs_copy(by).wait_recv())
-        zsum[...] = jnp.sum(zrecv[...], axis=0) + zsend[plane]
+        first = pl.multiple_of(plane * piece, 8)
+        zsum[...] = jnp.sum(zrecv[...].astype(F32), axis=0) + part[which, pl.ds(first, piece), :]
         grad[plane] = zsum[...]
         each(lambda by: ag_copy(by).start())
 
+    for i in range(PARTS // 2, PARTS):
+        pass_on(0, i)
+
+    for copy in w_copies:
+        copy.start()
+
+    @pl.when(x == 2)
+    def _():
+        for i in range(PARTS):
+            d1_copy(1, i, True).wait_recv()
+            right_copy(i).start()
+
     @pl.when(x == 0)
     def _():
-        for i in range(tiles):
-            d1_copy(0, i, True).wait_recv()
-            d2_copy(0, i).start()
-
-    for i in range(tiles):
-        d1_copy(1, i, True).wait_recv()
-
-    @pl.when(seq >= 1)
-    def _():
-        attend(kh.at[0], vh.at[0], 1)
-
-    for i in range(tiles):
-        d3_copy(0, i, True).wait_recv()
-
-    @pl.when(seq >= 3)
-    def _():
-        attend(kh.at[2], vh.at[2], 3)
+        for i in range(PARTS):
+            send_keys(i)
+
+    @pl.when(seq >= 4)
+    def _():
+        attend(kh.at[3], vh.at[3], 4)
 
     def bc_copy(by):
         return remote(new.at[which], new.at[which], bc_s.at[by - 1], bc_r.at[which], at_x(by))
@@ -361,12 +374,33 @@
             return carry
 
         lax.fori_loop(0, 5, sweep, 0)
-        new[which] = (weights[which].astype(F32) - part[0]).astype(BF16)
+        for m, old in enumerate((gate_w, up_w, down_w)):
+
+            @pl.when(x == m)
+            def _(m=m, old=old):
+                new[m] = (old[0].astype(F32) - part[0]).astype(BF16)
+
         for by in (1, 2, 3):
             bc_copy(by).start()
 
+    @pl.when(x != 2)
+    def _():
+        for i in range(PARTS):
+            d1_copy(1, i, True).wait_recv()
+
+    @pl.when(seq >= 1)
+    def _():
+        attend(kh.at[0], vh.at[0], 1)
+
+    for i in range(PARTS):
+        d3_copy(0, i, True).wait_recv()
+
+    @pl.when(seq >= 3)
+    def _():
+        attend(kh.at[2], vh.at[2], 3)
+
     for kind in (0, 1):
-        for i in range(tiles):
+        for i in range(PARTS):
             d2_copy(kind, i).wait_recv()
 
     @pl.when(seq >= 2)
@@ -422,11 +456,20 @@
         out[at, :] = mixed.astype(BF16)
 
     for kind in (0, 1):
-        for i in range(tiles):
+        for i in range(PARTS):
             row_copy(kind, i).wait_send()
             d1_copy(kind, i, True).wait_send()
-            d2_copy(kind, i).wait_send()
             d3_copy(kind, i, True).wait_send()
+    for i in range(PARTS):
+        d2_copy(0, i).wait_send()
+
+        @pl.when(x > 0)
+        def _():
+            d2_copy(1, i).wait_send()
+
+        @pl.when(x == 2)
+        def _():
+            right_copy(i).wait_send()
     for by in (1, 2, 3):
         m, copy = xs_copy(by)
 
@@ -450,7 +493,6 @@
 def shards(queries, keys, values, learn_rate, gate_fast, up_fast, down_fast, ttt_gain, out_weight):
     tok, hd = queries.shape
     tiles = tok // 256
-    weights = jnp.concatenate([gate_fast, up_fast, down_fast])
     piece = hd // PLANE
     dma = lambda n: pltpu.SemaphoreType.DMA((n,))
     scratch = [
@@ -466,8 +508,8 @@
         pltpu.VMEM((3, hd, hd), F32),
         pltpu.VMEM((3, hd, hd), BF16),
         pltpu.VMEM((3, hd, hd), BF16),
-        pltpu.VMEM((PLANE, piece, hd), F32),
-        pltpu.VMEM((PLANE - 1, piece, hd), F32),
+        pltpu.VMEM((PLANE, piece, hd), BF16),
+        pltpu.VMEM((PLANE - 1, piece, hd), BF16),
         pltpu.VMEM((piece, hd), F32),
         pltpu.VMEM((PLANE, piece, hd), F32),
         pltpu.VMEM((hd, 3 * hd), BF16),
@@ -477,21 +519,21 @@
         pltpu.VMEM((4, tok, hd), BF16),
         pltpu.VMEM((4, hd, hd), BF16),
     ]
-    scratch += [dma(2 * tiles)] * 8
+    scratch += [dma(2 * PARTS)] * 8 + [dma(PARTS)]
     scratch += [dma(3)] * 2 + [dma(PLANE - 1)] * 4 + [dma(3)] * 2
     scratch += [dma(3)] * 2 + [dma(tiles)] * 6
     vmem = pl.BlockSpec(memory_space=pltpu.VMEM)
     return pl.pallas_call(
         layer,
         out_shape=jax.ShapeDtypeStruct((tok, hd), BF16),
-        in_specs=[vmem] * 7,
+        in_specs=[vmem] * 9,
         out_specs=vmem,
         scratch_shapes=scratch,
         compiler_params=pltpu.CompilerParams(
             collective_id=0, has_side_effects=True, vmem_limit_bytes=56 * 1024 * 1024
         ),
         name="layer",
-    )(queries, keys, values, learn_rate, weights, ttt_gain, out_weight)
+    )(queries, keys, values, learn_rate, gate_fast, up_fast, down_fast, ttt_gain, out_weight)
 
 
 def solution(mesh):

time: 132 us -> 117 us (0.89)
  Pallas kernels: 127 us -> 114 us
  other arithmetic: 2.18 us -> 0 us
    pallas_call x1, Pallas kernels: 127 us -> 114 us  [shards(): pl.pallas_call(layer, out_shape=jax.ShapeDtypeStruct((tok, hd), BF16), in...]
    concatenate x1 -> x0, other arithmetic: 2.18 us -> none  [shards(): weights = jnp.concatenate([gate_fast, up_fast, down_fast])]
where the time goes in v1:
time: 117 us; the launch traced here: 116 us
  Pallas kernels  114 us (97%)
  local copies, waits for them, and re-layouts  1.94 us (2%)
    pallas_call x1, Pallas kernels, shards(): pl.pallas_call(layer, out_shape=jax.ShapeDtypeStruct((tok, hd), BF16), in...  114 us

profile of v1, /device:TPU:53, one launch (start us, length us, event | category | flops | bytes accessed | tf_op | source)
XLA Modules:
  0.0 116.4 jit_solution(9944056121842259902)
XLA Ops:
  0.0 114.5 %layer.1 = bf16[768,384]{1,0:T(8,128)(2,1)} custom-call(bf16[768,384]{1,0:T(8,128)(2,1)} %q.1, bf16[768,384]{1,0:T(8,128)(2,1)} %k.1, bf16[768,384]{1,0:T(8,128)(2,1)} %v.1, f32[1,768]{1,0:T(1,128)} %lr.1, bf16[1,384,384]{2,1,0:T(8,128)(2,1)} %gate_w.1, bf16[1,384,384]{2,1,0:T(8,128)(2,1)} %up_w.1, bf16[1,384,384]{2,1,0:T(8,128)(2,1)} %down_w.1, ...), custom_call_target="tpu_custom_call" | custom-call | tf_op jit(solution)/shard_map/layer/pallas_call | solution.py:526
  114.5 1.9 %copy.11 = bf16[768,384]{1,0:T(8,128)(2,1)} copy(bf16[768,384]{1,0:T(8,128)(2,1)} %layer.1) | data formatting | bytes 1179648

commit v2 on v1

--- a/solution.py
+++ b/solution.py
@@ -111,7 +111,7 @@
         return pl.ds(i * tile, tile)
 
     def span(i):
-        return pl.ds(i * chunk, chunk)
+        return pl.ds(i * chunk if isinstance(i, int) else pl.multiple_of(i * chunk, chunk), chunk)
 
     own = (k, v)
     held = (kh, vh)
@@ -262,6 +262,12 @@
         for i in range(PARTS):
             row_copy(kind, i).start()
 
+    @pl.when(x == 2)
+    def _():
+        for kind in (0, 1):
+            for i in range(PARTS):
+                d1_copy(kind, i, True).start()
+
     @pl.when(owner)
     def _():
         for by in (1, 2, 3):
@@ -271,7 +277,7 @@
         zsend[...] = whole.reshape(PLANE, piece, hd).astype(BF16)
         each(lambda by: zs_copy(by).start())
 
-    @pl.when(x < 3)
+    @pl.when(x < 2)
     def _():
         for kind in (0, 1):
             for i in range(PARTS):
@@ -317,20 +323,18 @@
     for copy in w_copies:
         copy.start()
 
+    def send_right(i):
+        d1_copy(1, i, True).wait_recv()
+        right_copy(i).start()
+
     @pl.when(x == 2)
     def _():
-        for i in range(PARTS):
-            d1_copy(1, i, True).wait_recv()
-            right_copy(i).start()
+        send_right(0)
 
     @pl.when(x == 0)
     def _():
         for i in range(PARTS):
             send_keys(i)
-
-    @pl.when(seq >= 4)
-    def _():
-        attend(kh.at[3], vh.at[3], 4)
 
     def bc_copy(by):
         return remote(new.at[which], new.at[which], bc_s.at[by - 1], bc_r.at[which], at_x(by))
@@ -371,6 +375,11 @@
             part[1] = ns_second * part[1] + ns_third * dot_nt(left[...], right[...])
             spread(part[1])
             part[0] = ns_first * part[0] + dot_nn(left[...], stack[...])
+
+            @pl.when(x == 2)
+            def _():
+                send_right(n + 1)
+
             return carry
 
         lax.fori_loop(0, 5, sweep, 0)
@@ -382,6 +391,10 @@
 
         for by in (1, 2, 3):
             bc_copy(by).start()
+
+    @pl.when(seq >= 4)
+    def _():
+        attend(kh.at[3], vh.at[3], 4)
 
     @pl.when(x != 2)
     def _():

time: 117 us -> 113 us (0.966)
  Pallas kernels: 114 us -> 111 us
    pallas_call x1, Pallas kernels: 114 us -> 111 us  [shards(): pl.pallas_call(layer, out_shape=jax.ShapeDtypeStruct((tok, hd), BF16), in...]
where the time goes in v2:
time: 113 us
  Pallas kernels  111 us (98%)
  local copies, waits for them, and re-layouts  1.94 us (2%)
    pallas_call x1, Pallas kernels, shards(): pl.pallas_call(layer, out_shape=jax.ShapeDtypeStruct((tok, hd), BF16), in...  111 us

profile of v2, /device:TPU:53, one launch (start us, length us, event | category | flops | bytes accessed | tf_op | source)
XLA Modules:
  0.0 113.1 jit_solution(3895365906695662374)
XLA Ops:
  0.0 111.1 %layer.1 = bf16[768,384]{1,0:T(8,128)(2,1)} custom-call(bf16[768,384]{1,0:T(8,128)(2,1)} %q.1, bf16[768,384]{1,0:T(8,128)(2,1)} %k.1, bf16[768,384]{1,0:T(8,128)(2,1)} %v.1, f32[1,768]{1,0:T(1,128)} %lr.1, bf16[1,384,384]{2,1,0:T(8,128)(2,1)} %gate_w.1, bf16[1,384,384]{2,1,0:T(8,128)(2,1)} %up_w.1, bf16[1,384,384]{2,1,0:T(8,128)(2,1)} %down_w.1, ...), custom_call_target="tpu_custom_call" | custom-call | tf_op jit(solution)/shard_map/layer/pallas_call | solution.py:539
  111.1 1.9 %copy.11 = bf16[768,384]{1,0:T(8,128)(2,1)} copy(bf16[768,384]{1,0:T(8,128)(2,1)} %layer.1) | data formatting | bytes 1179648

commit v3 on v2

--- a/solution.py
+++ b/solution.py
@@ -243,8 +243,8 @@
         return remote(zsum, grad.at[plane], ag_s.at[by - 1], ag_r.at[by - 1], at_plane(by))
 
     def each(fn):
-        def go(by, carry):
-            fn(by)
+        def go(n, carry):
+            fn(lax.rem(n + PLANE // 2 - 2, PLANE - 1) + 1)
             return carry
 
         lax.fori_loop(1, PLANE, go, 0)

time: 113 us -> 114 us (level)
  no operation moved by 1% of the time
where the time goes in v3:
time: 114 us; the launch traced here: 113 us
  Pallas kernels  111 us (97%)
  local copies, waits for them, and re-layouts  1.94 us (2%)
    pallas_call x1, Pallas kernels, shards(): pl.pallas_call(layer, out_shape=jax.ShapeDtypeStruct((tok, hd), BF16), in...  111 us

profile of v3, /device:TPU:53, one launch (start us, length us, event | category | flops | bytes accessed | tf_op | source)
XLA Modules:
  0.0 113.4 jit_solution(3310132738507957783)
XLA Ops:
  0.0 111.5 %layer.1 = bf16[768,384]{1,0:T(8,128)(2,1)} custom-call(bf16[768,384]{1,0:T(8,128)(2,1)} %q.1, bf16[768,384]{1,0:T(8,128)(2,1)} %k.1, bf16[768,384]{1,0:T(8,128)(2,1)} %v.1, f32[1,768]{1,0:T(1,128)} %lr.1, bf16[1,384,384]{2,1,0:T(8,128)(2,1)} %gate_w.1, bf16[1,384,384]{2,1,0:T(8,128)(2,1)} %up_w.1, bf16[1,384,384]{2,1,0:T(8,128)(2,1)} %down_w.1, ...), custom_call_target="tpu_custom_call" | custom-call | tf_op jit(solution)/shard_map/layer/pallas_call | solution.py:539
  111.5 1.9 %copy.11 = bf16[768,384]{1,0:T(8,128)(2,1)} copy(bf16[768,384]{1,0:T(8,128)(2,1)} %layer.1) | data formatting | bytes 1179648
